TPU v7x, 32 devices: a whole 2x2x4 slice. The times are simulated.
32 devices in a mesh: tilt: 2 (over y), dom: 16 (over z, x, core).
Axes of the slice: x: 2, y: 2, z: 4, core: 2. Of those that a mesh axis runs over, the one named last changes fastest.
Arguments:
- sections: bfloat16 [32, 256, 256], P('dom'), may hold values from -6 to 6
- images: bfloat16 [32, 4, 256, 256], P('dom', 'tilt'), may hold values from -6 to 6
- slice_rows: bfloat16 [4, 256, 256], P('tilt'), may hold values from -0.375 to 0.375
- slice_cols: bfloat16 [4, 256, 256], P('tilt'), may hold values from -0.375 to 0.375
- ctf_filter: bfloat16 [4, 256, 256], P('tilt'), may hold values from -0.375 to 0.375
- nbr_owner: int32 [32, 2, 8], P('dom'), may hold values from 0 to 15, all different within a row; in each aligned block of 4 rows (0 to 3, 4 to 7, ..., all dimensions but the last counted through in order) at most 4 rows name the same one
- nbr_local: int32 [32, 16], P('dom'), may hold values from 0 to 1
- nbr_side: int32 [32, 16], P('dom'), may hold values from 0 to 1
- nbr_weight: float32 [32, 16], P('dom'), may hold values from 0.25 to 2
Outputs:
- section_grad: float32 [32, 256, 256], P('dom', 'tilt')
- scores: float32 [32], P('dom')
Inputs may be any that keep to these rules, and one draw needn't show every extreme that they name: `nbr_owner`: among the 32 neighbour entries of one spatial block's particles, at most 4 name the same owner block; some blocks reach 4.
All inputs are finite; a program needn't handle non-finite values.
Results may differ from a plain program's by a relative error of at most 0.013.
Values may be sent and summed in bfloat16 or wider, within the bound.
No kernel may reach another device: no remote copies, remote signals or barrier semaphores. Data moves between devices by JAX's collectives and lax.ppermute only.
A program may use at most 64 MiB of HBM per device.

v0:
```python
import jax
import jax.numpy as jnp
from jax import lax
from jax.sharding import PartitionSpec as P

OVL = 16


def split_dot(weights, bands):
    hi = weights.astype(jnp.bfloat16)
    rest = weights - hi.astype(jnp.float32)
    mid = rest.astype(jnp.bfloat16)
    low = (rest - mid.astype(jnp.float32)).astype(jnp.bfloat16)
    total = jnp.dot(hi, bands, preferred_element_type=jnp.float32)
    total = total + jnp.dot(mid, bands, preferred_element_type=jnp.float32)
    return total + jnp.dot(low, bands, preferred_element_type=jnp.float32)


def on_device(
    sections, images, slice_rows, slice_cols, ctf_filter, nbr_owner, nbr_local, nbr_side, nbr_weight
):
    own_count = sections.shape[0]
    pixels = sections.shape[1]
    tilt_count = images.shape[1]
    neighbours = nbr_local.shape[1]
    peer_count = lax.axis_size("dom")
    total = own_count * peer_count
    me = lax.axis_index("dom")
    band_size = tilt_count * OVL * pixels
    target = nbr_owner.reshape(own_count, neighbours) * own_count + nbr_local
    every = jnp.arange(total)
    hits = target[:, :, None] == every[None, None, :]
    fwd = [
        jnp.sum(jnp.where(hits & (nbr_side == s)[:, :, None], nbr_weight[:, :, None], 0.0), axis=1)
        for s in (0, 1)
    ]
    target_all = lax.all_gather(target, "dom", axis=0, tiled=True)
    side_all = lax.all_gather(nbr_side, "dom", axis=0, tiled=True)
    weight_all = lax.all_gather(nbr_weight, "dom", axis=0, tiled=True)
    halfway = jnp.einsum(
        "kij,tlj->ktil", sections, slice_cols, preferred_element_type=jnp.float32
    ).astype(jnp.bfloat16)
    projected = jnp.einsum(
        "tai,ktil->ktal", slice_rows, halfway, preferred_element_type=jnp.float32
    ).astype(jnp.bfloat16)
    edges = jnp.stack((projected[:, :, :OVL], projected[:, :, pixels - OVL :]), axis=1)
    edges_all = lax.all_gather(edges, "dom", axis=0, tiled=True)
    lower_part = split_dot(fwd[0], edges_all[:, 0].reshape(total, band_size))
    upper_part = split_dot(fwd[1], edges_all[:, 1].reshape(total, band_size))
    lower_part = lower_part.reshape(own_count, tilt_count, OVL, pixels)
    upper_part = upper_part.reshape(own_count, tilt_count, OVL, pixels)
    residual = images.astype(jnp.float32) - projected.astype(jnp.float32)
    residual = residual.at[:, :, :OVL].add(-upper_part)
    residual = residual.at[:, :, pixels - OVL :].add(-lower_part)
    residual_portion = residual.astype(jnp.bfloat16)
    smoothed_images = jnp.einsum(
        "tab,ktbc->ktac", ctf_filter, residual_portion, preferred_element_type=jnp.float32
    ).astype(jnp.bfloat16)
    filtered_images = jnp.einsum(
        "ktac,tdc->ktad", smoothed_images, ctf_filter, preferred_element_type=jnp.float32
    )
    score_part = jnp.sum(filtered_images * filtered_images, axis=(1, 2, 3))
    tilt_groups = lax.axis_size("tilt")
    scores = 0.5 * lax.psum(score_part, "tilt") / (tilt_count * tilt_groups * pixels * pixels)
    filtered_portion = filtered_images.astype(jnp.bfloat16)
    reverse_pass = jnp.einsum(
        "tab,ktac->ktbc", ctf_filter, filtered_portion, preferred_element_type=jnp.float32
    ).astype(jnp.bfloat16)
    weighted = jnp.einsum(
        "ktbc,tcd->ktbd", reverse_pass, ctf_filter, preferred_element_type=jnp.float32
    ).astype(jnp.bfloat16)
    grad_bands = jnp.stack((weighted[:, :, :OVL], weighted[:, :, pixels - OVL :]), axis=1)
    grad_all = lax.all_gather(grad_bands, "dom", axis=0, tiled=True)
    mine = me * own_count + jnp.arange(own_count)
    named = target_all[None, :, :] == mine[:, None, None]
    back = [
        jnp.sum(jnp.where(named & (side_all == s)[None], weight_all[None], 0.0), axis=2)
        for s in (0, 1)
    ]
    add_top = split_dot(back[0], grad_all[:, 1].reshape(total, band_size))
    add_bottom = split_dot(back[1], grad_all[:, 0].reshape(total, band_size))
    add_top = add_top.reshape(own_count, tilt_count, OVL, pixels)
    add_bottom = add_bottom.reshape(own_count, tilt_count, OVL, pixels)
    proj_grad = weighted.astype(jnp.float32)
    proj_grad = proj_grad.at[:, :, :OVL].add(add_top)
    proj_grad = proj_grad.at[:, :, pixels - OVL :].add(add_bottom)
    proj_half = proj_grad.astype(jnp.bfloat16)
    upward = jnp.einsum(
        "tai,ktal->ktil", slice_rows, proj_half, preferred_element_type=jnp.float32
    ).astype(jnp.bfloat16)
    partial_grad = -jnp.einsum(
        "ktil,tlj->kij", upward, slice_cols, preferred_element_type=jnp.float32
    )
    section_grad = lax.psum_scatter(partial_grad, "tilt", scatter_dimension=1, tiled=True)
    return (section_grad, scores)


def solution(mesh):
    in_specs = (
        P("dom", None, None),
        P("dom", "tilt", None, None),
        P("tilt", None, None),
        P("tilt", None, None),
        P("tilt", None, None),
        P("dom", None, None),
        P("dom", None),
        P("dom", None),
        P("dom", None),
    )
    out_specs = (P("dom", "tilt", None), P("dom"))
    return jax.shard_map(
        on_device, mesh=mesh, in_specs=in_specs, out_specs=out_specs, check_vma=False
    )
```

profile of v0, /device:TPU:0, one launch (start us, length us, event | category | flops | bytes accessed | tf_op | source)
XLA Modules:
  0.0 136.8 jit_solution(1483881849874437)
XLA Ops:
  7.2 1.9 %convert_subtract_fusion = (f32[2,2,256,256]{3,2,0,1:T(8,128)S(1)}, bf16[2,2,256,256]{3,2,0,1:T(8,128)(2,1)S(1)}) fusion(bf16[2,2,256,256]{3,2,1,0:T(8,128)(2,1)} %param.18, bf16[2,256,256]{2,1,0:T(8,128)(2,1)} %param.19, bf16[2,256,256]{2,1,0:T(8,128)(2,1)} %param.20, bf16[2,256,256]{2,1,0:T(8,128)(2,1)} %param.17), kind=kOutput, calls=%fused_computation.26 | convolution fusion | flops 269746176 | bytes 2883584 | tf_op jit(solution)/shard_map/tai,ktil->ktal/dot_general | solution.py:43
  9.1 0.6 pad_maximum_fusion
  9.8 0.6 copy-done.5
  10.5 0.6 copy-done.6
  11.1 0.7 copy-done.4
  11.8 0.7 copy-done.3
  12.6 38.9 %all-gather.6.cloned.1.call-done = bf16[32,2,2,16,256]{4,3,0,2,1:T(8,128)(2,1)} async-done(((bf16[2,2,2,16,256]{4,3,0,2,1:T(8,128)(2,1)}), bf16[32,2,2,16,256]{4,3,0,2,1:T(8,128)(2,1)}) %all-gather.6.cloned.1.call-update) | async-done | bytes 1048592 | tf_op jit(solution)/shard_map/all_gather | solution.py:47
  51.5 1.3 fusion.53
  52.8 0.2 reshape_squeeze.12
  53.2 0.2 convolution_add_fusion.7
  53.4 0.2 fusion.1
  53.7 0.2 reshape_squeeze.13
  54.1 0.2 convolution_add_fusion.5
  54.3 0.2 fusion
  54.6 0.7 multiply_reduce_fusion
  55.3 0.6 fusion.58
  55.9 0.6 pad_maximum_fusion.1
  56.7 19.3 %all-gather.2 = f32[16,2,16]{2,1,0:T(2,128)S(1)} all-gather(f32[1,2,16]{2,1,0:T(2,128)S(1)} %bitcast.146), channel_id=1, replica_groups=mesh['tilt'=2,'dom'=16] {'dom'}, dimensions={0}, use_global_device_ids=true | all-gather | bytes 2176 | tf_op jit(solution)/shard_map/all_gather | solution.py:39
  76.1 17.4 %all-gather = s32[16,2,16]{2,1,0:T(2,128)S(1)} all-gather(s32[1,2,16]{2,1,0:T(2,128)S(1)} %bitcast.145), channel_id=1, replica_groups=mesh['tilt'=2,'dom'=16] {'dom'}, dimensions={0}, use_global_device_ids=true | all-gather | bytes 2176 | tf_op jit(solution)/shard_map/all_gather | solution.py:37
  93.5 18.8 %all-gather.1 = s32[16,2,16]{2,1,0:T(2,128)S(1)} all-gather(s32[1,2,16]{2,1,0:T(2,128)S(1)} %bitcast.147), channel_id=1, replica_groups=mesh['tilt'=2,'dom'=16] {'dom'}, dimensions={0}, use_global_device_ids=true | all-gather | bytes 2176 | tf_op jit(solution)/shard_map/all_gather | solution.py:38
  112.7 1.3 fusion.52
  114.0 0.2 reshape_squeeze.14
  114.5 0.2 convolution_add_fusion.3
  114.7 0.2 convolution_add_fusion.2
  114.9 0.2 reshape_squeeze.15
  115.4 0.2 convolution_add_fusion.1
  115.6 0.2 convolution_add_fusion
  115.9 0.9 copy-done.1
  116.8 1.5 %fusion.9 = f32[2,256,256]{2,1,0:T(8,128)} fusion(bf16[2,256,256]{2,1,0:T(8,128)(2,1)S(1)} %copy-done.1, bf16[2,256,256]{2,1,0:T(8,128)(2,1)S(1)} %copy-done.2, f32[2,2,256,256]{3,2,0,1:T(8,128)S(1)} %fusion.30), kind=kOutput, calls=%fused_computation.24 | convolution fusion | flops 269090816 | bytes 2097152 | tf_op jit(solution)/shard_map/ktil,tlj->kij/dot_general | solution.py:91
  118.3 4.9 %psum.7 = f32[2]{0:T(128)S(1)} all-reduce(f32[2]{0:T(128)S(1)} %get-tuple-element.70), channel_id=1, replica_groups=mesh['tilt'=2,'dom'=16] {'tilt'}, use_global_device_ids=true, to_apply=%region_6.7 | all-reduce | flops 2 | bytes 16 | tf_op jit(solution)/shard_map/psum | solution.py:64
  123.3 0.5 broadcast_multiply_fusion.1
  123.8 6.5 %reduce-scatter.2.cloned.1.call-done = f32[2,128,256]{2,1,0:T(8,128)} async-done(((f32[2,256,256]{2,1,0:T(8,128)}), f32[2,128,256]{2,1,0:T(8,128)}) %reduce-scatter.2.cloned.1.call-update) | async-done | bytes 262160 | tf_op jit(solution)/shard_map/reduce_scatter | solution.py:94
  (48 shorter events, 2.0 us)
Async XLA Ops:
  7.2 47.4 %copy-start = (bf16[2,256,256]{2,1,0:T(8,128)(2,1)S(1)}, bf16[2,256,256]{2,1,0:T(8,128)(2,1)}, u32[]{:S(2)}) copy-start(bf16[2,256,256]{2,1,0:T(8,128)(2,1)} %param.21) | copy-start | bytes 786436
  7.2 44.3 %all-gather.6.cloned.1.call-start = ((), (), s32[]{:S(2)}) async-start(), calls=%async_computation.1 | async-start | bytes 1114112 | tf_op jit(solution)/shard_map/all_gather | solution.py:47
  9.7 0.7 copy-start.5
  9.8 102.9 %all-gather.8.cloned.1.call-start = ((), (), s32[]{:S(2)}) async-start(), calls=%async_computation.2 | async-start | bytes 1114112 | tf_op jit(solution)/shard_map/all_gather | solution.py:73
  10.4 0.7 copy-start.6
  11.1 0.7 copy-start.4
  11.8 0.7 copy-start.3
  56.6 73.7 %reduce-scatter.2.cloned.1.call-start = ((), (), s32[]{:S(2)}) async-start(), calls=%async_computation.3 | async-start | bytes 786432 | tf_op jit(solution)/shard_map/reduce_scatter | solution.py:94
  115.8 1.0 copy-start.1
  115.8 1.0 copy-start.2
Sparse Core Ops, SparseCore 0:
  10.8 40.6 all-gather.5
  56.7 36.8 all-gather.7
  118.5 11.8 reduce-scatter.1
where the time goes:
time: 137 us
  blocking collectives  60.5 us (44%)
  waiting for transfers between devices  45.5 us (33%)
  between operations  14 us (10%)
  local copies, waits for them, and re-layouts  7.73 us (6%)
  matrix products  6.92 us (5%)
  other arithmetic  2.08 us (2%)
    all_gather x1, waiting for transfers between devices, on_device(): edges_all = lax.all_gather(edges, 'dom', axis=0, tiled=True)  38.9 us
    all_gather x1, blocking collectives, on_device(): weight_all = lax.all_gather(nbr_weight, 'dom', axis=0, tiled=True)  19.3 us
    all_gather x1, blocking collectives, on_device(): side_all = lax.all_gather(nbr_side, 'dom', axis=0, tiled=True)  18.8 us
    all_gather x1, blocking collectives, on_device(): target_all = lax.all_gather(target, 'dom', axis=0, tiled=True)  17.4 us
    reduce_scatter x1, waiting for transfers between devices, on_device(): lax.psum_scatter(partial_grad, 'tilt', scatter_dimension=1, tiled=True)  6.51 us
    psum x1, blocking collectives, on_device(): lax.psum(score_part, 'tilt')  4.94 us
    unnamed x20, local copies, waits for them, and re-layouts  3.68 us
  transfers between devices with their start and end apart: 3, of which 2 were waited for; matrix products, arithmetic and copies ran while one was open for 1% of the time, Pallas kernels for 0%

commit v1 on v0

--- a/solution.py
+++ b/solution.py
@@ -4,6 +4,23 @@
 from jax.sharding import PartitionSpec as P
 
 OVL = 16
+
+
+def laid_out(blocks, dim):
+    shape = list(blocks.shape[1:])
+    shape[dim] *= blocks.shape[0]
+    return jnp.moveaxis(blocks, 0, dim).reshape(shape)
+
+
+def grow_blocks(x, axis):
+    count, mine = (lax.axis_size(axis), lax.axis_index(axis))
+    tiles, bit = (x[None], 1)
+    while bit < count:
+        other = lax.ppermute(tiles, axis, [(i, i ^ bit) for i in range(count)])
+        low = mine & bit == 0
+        tiles = jnp.concatenate([jnp.where(low, tiles, other), jnp.where(low, other, tiles)])
+        bit *= 2
+    return tiles
 
 
 def split_dot(weights, bands):
@@ -36,7 +53,7 @@
     ]
     target_all = lax.all_gather(target, "dom", axis=0, tiled=True)
     side_all = lax.all_gather(nbr_side, "dom", axis=0, tiled=True)
-    weight_all = lax.all_gather(nbr_weight, "dom", axis=0, tiled=True)
+    weight_all = laid_out(grow_blocks(nbr_weight, "dom"), 0)
     halfway = jnp.einsum(
         "kij,tlj->ktil", sections, slice_cols, preferred_element_type=jnp.float32
     ).astype(jnp.bfloat16)

time: 137 us -> 128 us (0.934)
  blocking collectives: 60.5 us -> 43.1 us
  waiting for transfers between devices: 45.5 us -> 52.6 us
    all_gather x1 -> x0, blocking collectives: 19.3 us -> none  [on_device(): weight_all = lax.all_gather(nbr_weight, 'dom', axis=0, tiled=True)]
    ppermute x0 -> x4, waiting for transfers between devices: none -> 7.11 us  [grow_blocks(): other = lax.ppermute(tiles, axis, [(i, i ^ bit) for i in range(count)])]
    all_gather x1, blocking collectives: 17.4 us -> 18.9 us  [on_device(): target_all = lax.all_gather(target, 'dom', axis=0, tiled=True)]
    unnamed x20 -> x19, local copies, waits for them, and re-layouts: 3.68 us -> 3.61 us
  transfers between devices with their start and end apart: 3 -> 7, of which waited for: 2 -> 4; matrix products, arithmetic and copies ran while one was open for 1% -> 1% of each run, Pallas kernels for 0% -> 0%
where the time goes in v1:
time: 128 us; the launch traced here: 127 us
  waiting for transfers between devices  52.6 us (41%)
  blocking collectives  43.1 us (34%)
  between operations  14.1 us (11%)
  local copies, waits for them, and re-layouts  7.73 us (6%)
  matrix products  6.92 us (5%)
  other arithmetic  2.15 us (2%)
    all_gather x1, waiting for transfers between devices, on_device(): edges_all = lax.all_gather(edges, 'dom', axis=0, tiled=True)  38.9 us
    all_gather x1, blocking collectives, on_device(): side_all = lax.all_gather(nbr_side, 'dom', axis=0, tiled=True)  19.3 us
    all_gather x1, blocking collectives, on_device(): target_all = lax.all_gather(target, 'dom', axis=0, tiled=True)  18.9 us
    ppermute x4, waiting for transfers between devices, grow_blocks(): other = lax.ppermute(tiles, axis, [(i, i ^ bit) for i in range(count)])  7.11 us
    reduce_scatter x1, waiting for transfers between devices, on_device(): lax.psum_scatter(partial_grad, 'tilt', scatter_dimension=1, tiled=True)  6.51 us
    psum x1, blocking collectives, on_device(): lax.psum(score_part, 'tilt')  4.94 us
    unnamed x19, local copies, waits for them, and re-layouts  3.61 us
  transfers between devices with their start and end apart: 7, of which 4 were waited for; matrix products, arithmetic and copies ran while one was open for 1% of the time, Pallas kernels for 0%

profile of v1, /device:TPU:0, one launch (start us, length us, event | category | flops | bytes accessed | tf_op | source)
XLA Modules:
  0.0 127.3 jit_solution(13239194027943825999)
XLA Ops:
  7.2 1.9 %convert_subtract_fusion = (f32[2,2,256,256]{3,2,0,1:T(8,128)S(1)}, bf16[2,2,256,256]{3,2,0,1:T(8,128)(2,1)S(1)}) fusion(bf16[2,2,256,256]{3,2,1,0:T(8,128)(2,1)} %param.18, bf16[2,256,256]{2,1,0:T(8,128)(2,1)} %param.19, bf16[2,256,256]{2,1,0:T(8,128)(2,1)} %param.20, bf16[2,256,256]{2,1,0:T(8,128)(2,1)} %param.17), kind=kOutput, calls=%fused_computation.26 | convolution fusion | flops 269746176 | bytes 2883584 | tf_op jit(solution)/shard_map/tai,ktil->ktal/dot_general | solution.py:60
  9.1 0.6 pad_maximum_fusion
  9.8 0.6 copy-done.5
  10.5 0.6 copy-done.6
  11.1 0.7 copy-done.3
  11.8 0.7 copy-done.4
  12.6 38.9 %all-gather.5.cloned.1.call-done = bf16[32,2,2,16,256]{4,3,0,2,1:T(8,128)(2,1)} async-done(((bf16[2,2,2,16,256]{4,3,0,2,1:T(8,128)(2,1)}), bf16[32,2,2,16,256]{4,3,0,2,1:T(8,128)(2,1)}) %all-gather.5.cloned.1.call-update) | async-done | bytes 1048592 | tf_op jit(solution)/shard_map/all_gather | solution.py:64
  51.5 1.3 fusion.53
  52.8 0.2 reshape_squeeze.12
  53.2 0.2 convolution_add_fusion.7
  53.4 0.2 fusion.1
  53.7 0.2 reshape_squeeze.13
  54.1 0.2 convolution_add_fusion.5
  54.3 0.2 fusion
  54.6 0.7 multiply_reduce_fusion
  55.3 0.6 fusion.58
  55.9 0.6 pad_maximum_fusion.1
  56.7 0.3 collective-permute-start
  57.0 19.3 %all-gather.1 = s32[16,2,16]{2,1,0:T(2,128)S(1)} all-gather(s32[1,2,16]{2,1,0:T(2,128)S(1)} %bitcast.148), channel_id=1, replica_groups=mesh['tilt'=2,'dom'=16] {'dom'}, dimensions={0}, use_global_device_ids=true | all-gather | bytes 2176 | tf_op jit(solution)/shard_map/all_gather | solution.py:55
  76.4 3.5 %collective-permute-done.1 = f32[2,2,16]{2,1,0:T(2,128)S(1)} collective-permute-done((f32[2,2,16]{2,1,0:T(2,128)S(1)}, f32[2,2,16]{2,1,0:T(2,128)S(1)}, u32[]{:S(2)}, u32[]{:S(2)}) %collective-permute-start.1) | collective-permute-done | bytes 288 | tf_op jit(solution)/shard_map/ppermute | solution.py:19
  80.1 3.6 %collective-permute-done.2 = f32[4,2,16]{2,1,0:T(2,128)S(1)} collective-permute-done((f32[4,2,16]{2,1,0:T(2,128)S(1)}, f32[4,2,16]{2,1,0:T(2,128)S(1)}, u32[]{:S(2)}, u32[]{:S(2)}) %collective-permute-start.2) | collective-permute-done | bytes 544 | tf_op jit(solution)/shard_map/ppermute | solution.py:19
  83.8 18.9 %all-gather = s32[16,2,16]{2,1,0:T(2,128)S(1)} all-gather(s32[1,2,16]{2,1,0:T(2,128)S(1)} %bitcast.147), channel_id=1, replica_groups=mesh['tilt'=2,'dom'=16] {'dom'}, dimensions={0}, use_global_device_ids=true | all-gather | bytes 2176 | tf_op jit(solution)/shard_map/all_gather | solution.py:54
  103.2 1.3 fusion.52
  104.5 0.2 reshape_squeeze.14
  104.9 0.2 convolution_add_fusion.3
  105.4 0.2 reshape_squeeze.15
  105.8 0.2 convolution_add_fusion.1
  106.3 0.9 copy-done.1
  107.2 1.5 %fusion.9 = f32[2,256,256]{2,1,0:T(8,128)} fusion(bf16[2,256,256]{2,1,0:T(8,128)(2,1)S(1)} %copy-done.1, bf16[2,256,256]{2,1,0:T(8,128)(2,1)S(1)} %copy-done.2, f32[2,2,256,256]{3,2,0,1:T(8,128)S(1)} %fusion.30), kind=kOutput, calls=%fused_computation.24 | convolution fusion | flops 269090816 | bytes 2097152 | tf_op jit(solution)/shard_map/ktil,tlj->kij/dot_general | solution.py:108
  108.8 4.9 %psum.7 = f32[2]{0:T(128)S(1)} all-reduce(f32[2]{0:T(128)S(1)} %get-tuple-element.78), channel_id=1, replica_groups=mesh['tilt'=2,'dom'=16] {'tilt'}, use_global_device_ids=true, to_apply=%region_6.7 | all-reduce | flops 2 | bytes 16 | tf_op jit(solution)/shard_map/psum | solution.py:81
  113.7 0.5 broadcast_multiply_fusion.1
  114.2 6.5 %reduce-scatter.2.cloned.1.call-done = f32[2,128,256]{2,1,0:T(8,128)} async-done(((f32[2,256,256]{2,1,0:T(8,128)}), f32[2,128,256]{2,1,0:T(8,128)}) %reduce-scatter.2.cloned.1.call-update) | async-done | bytes 262160 | tf_op jit(solution)/shard_map/reduce_scatter | solution.py:111
  (63 shorter events, 2.7 us)
Async XLA Ops:
  7.2 47.4 %copy-start = (bf16[2,256,256]{2,1,0:T(8,128)(2,1)S(1)}, bf16[2,256,256]{2,1,0:T(8,128)(2,1)}, u32[]{:S(2)}) copy-start(bf16[2,256,256]{2,1,0:T(8,128)(2,1)} %param.21) | copy-start | bytes 786436
  7.2 44.3 %all-gather.5.cloned.1.call-start = ((), (), s32[]{:S(2)}) async-start(), calls=%async_computation.1 | async-start | bytes 1114112 | tf_op jit(solution)/shard_map/all_gather | solution.py:64
  9.7 0.7 copy-start.5
  9.8 93.4 %all-gather.7.cloned.1.call-start = ((), (), s32[]{:S(2)}) async-start(), calls=%async_computation.2 | async-start | bytes 1114112 | tf_op jit(solution)/shard_map/all_gather | solution.py:90
  10.4 0.7 copy-start.6
  11.1 0.7 copy-start.3
  11.8 0.7 copy-start.4
  56.6 64.2 %reduce-scatter.2.cloned.1.call-start = ((), (), s32[]{:S(2)}) async-start(), calls=%async_computation.3 | async-start | bytes 786432 | tf_op jit(solution)/shard_map/reduce_scatter | solution.py:111
  56.7 19.6 %collective-permute-start = (f32[1,2,16]{2,1,0:T(2,128)S(1)}, f32[1,2,16]{2,1,0:T(2,128)S(1)}, u32[]{:S(2)}, u32[]{:S(2)}) collective-permute-start(f32[1,2,16]{2,1,0:T(2,128)S(1)} %bitcast.149), channel_id=1, source_target_pairs={{0,1},{1,0},{2,3},{3,2},{4,5},{5,4},{6,7},{7,6},{8,9},{9,8},{10,11... | collective-permute-start | bytes 392 | tf_op jit(solution)/shard_map/ppermute | solution.py:19
  76.3 3.6 %collective-permute-start.1 = (f32[2,2,16]{2,1,0:T(2,128)S(1)}, f32[2,2,16]{2,1,0:T(2,128)S(1)}, u32[]{:S(2)}, u32[]{:S(2)}) collective-permute-start(f32[2,2,16]{2,1,0:T(2,128)S(1)} %pad_maximum_fusion.5), channel_id=1, source_target_pairs={{0,2},{1,3},{2,0},{3,1},{4,6},{5,7},{6,4},{7,5},{8,10},{9,11},{10,... | collective-permute-start | bytes 776 | tf_op jit(solution)/shard_map/ppermute | solution.py:19
  80.0 3.7 %collective-permute-start.2 = (f32[4,2,16]{2,1,0:T(2,128)S(1)}, f32[4,2,16]{2,1,0:T(2,128)S(1)}, u32[]{:S(2)}, u32[]{:S(2)}) collective-permute-start(f32[4,2,16]{2,1,0:T(2,128)S(1)} %pad_maximum_fusion.4), channel_id=1, source_target_pairs={{0,4},{1,5},{2,6},{3,7},{4,0},{5,1},{6,2},{7,3},{8,12},{9,13},{10,... | collective-permute-start | bytes 1544 | tf_op jit(solution)/shard_map/ppermute | solution.py:19
  83.7 19.2 %collective-permute-start.3 = (f32[8,2,16]{2,1,0:T(2,128)S(1)}, f32[8,2,16]{2,1,0:T(2,128)S(1)}, u32[]{:S(2)}, u32[]{:S(2)}) collective-permute-start(f32[8,2,16]{2,1,0:T(2,128)S(1)} %pad_maximum_fusion.3), channel_id=1, source_target_pairs={{0,8},{1,9},{2,10},{3,11},{4,12},{5,13},{6,14},{7,15},{8,0},{9,1},... | collective-permute-start | bytes 3080 | tf_op jit(solution)/shard_map/ppermute | solution.py:19
  106.2 1.0 copy-start.1
  106.2 1.0 copy-start.2
Sparse Core Ops, SparseCore 0:
  10.8 40.6 all-gather.4
  56.7 36.8 all-gather.6
  108.9 11.8 reduce-scatter.1
